TPU v7x, 512 devices: a whole 4x4x16 slice. The times are simulated.
512 devices in a mesh: region: 16 (over z), slab: 32 (over x, y, core).
Axes of the slice: x: 4, y: 4, z: 16, core: 2. Of those that a mesh axis runs over, the one named last changes fastest.
Arguments:
- records: bfloat16 [16384, 4096], P('region', 'slab'), may hold values from -6 to 6
- first_station: int32 [65536], P(('region', 'slab')), may hold values from 0 to 1023
- second_region: int32 [65536, 1], P(('region', 'slab')), may hold values from 0 to 15; in each aligned block of 128 rows (0 to 127, 128 to 255, ...) at most 16 rows name the same one
- second_station: int32 [65536], P(('region', 'slab')), may hold values from 0 to 1023
Outputs:
- stacks: bfloat16 [65536, 2048], P(('region', 'slab'))
Inputs may be any that keep to these rules, and one draw needn't show every extreme that they name: `second_region`: no region is named by more than 16 pairs of one device.
All inputs are finite; a program needn't handle non-finite values.
Results may differ from a plain program's by a relative error of at most 0.0077.
Values may be sent and summed in bfloat16 or wider, within the bound.
A program may use at most 64 MiB of HBM per device.

v0:
```python
import math
import jax
import jax.numpy as jnp
from jax import lax
from jax.sharding import PartitionSpec as P

NFFT = 2048
BINS = 1024
SEG = 2
HALF = 4


def dft_table():
    sample = jnp.arange(NFFT, dtype=jnp.int32)[:, None]
    frequency = jnp.arange(BINS, dtype=jnp.int32)[None, :]
    phase = (sample * frequency % NFFT).astype(jnp.float32) * (2.0 * math.pi / NFFT)
    return jnp.concatenate([jnp.cos(phase), -jnp.sin(phase)], axis=1).astype(jnp.bfloat16)


def whitened(traces):
    count = traces.shape[0]
    signal = traces.astype(jnp.float32).reshape(count * SEG, NFFT)
    signal = signal - jnp.mean(signal, axis=1, keepdims=True)
    position = jnp.arange(NFFT, dtype=jnp.int32).astype(jnp.float32)
    taper = 0.5 - 0.5 * jnp.cos(position * (2.0 * math.pi / NFFT))
    tapered = (signal * taper[None, :]).astype(jnp.bfloat16)
    spectrum = jnp.dot(tapered, dft_table(), preferred_element_type=jnp.float32)
    real_part = spectrum[:, :BINS]
    imag_part = spectrum[:, BINS:]
    amplitude = jnp.sqrt(real_part * real_part + imag_part * imag_part + 1e-06)
    padded = jnp.pad(amplitude, ((0, 0), (HALF, HALF)))
    smooth = jnp.zeros_like(amplitude)
    for offset in range(2 * HALF + 1):
        smooth = smooth + padded[:, offset : offset + BINS]
    smooth = smooth / (2 * HALF + 1)
    level = jnp.mean(amplitude, axis=1, keepdims=True)
    divisor = smooth + level + 1e-06
    white = spectrum / jnp.concatenate([divisor, divisor], axis=1)
    return white.astype(jnp.bfloat16).reshape(count, SEG * NFFT)


def cross(first_rows, second_rows):
    left = first_rows.astype(jnp.float32).reshape(first_rows.shape[:-1] + (SEG, 2, BINS))
    right = second_rows.astype(jnp.float32).reshape(second_rows.shape[:-1] + (SEG, 2, BINS))
    real_sum = jnp.mean(
        left[..., 0, :] * right[..., 0, :] + left[..., 1, :] * right[..., 1, :], axis=-2
    )
    imag_sum = jnp.mean(
        left[..., 0, :] * right[..., 1, :] - left[..., 1, :] * right[..., 0, :], axis=-2
    )
    return jnp.concatenate([real_sum, imag_sum], axis=-1).astype(jnp.bfloat16)


def local(records, first_station, second_region, second_station):
    regions = lax.axis_size("region")
    pair_count = first_station.shape[0]
    capacity = max(2, pair_count // regions + pair_count // 16)
    arrived = lax.all_to_all(records, "slab", split_axis=0, concat_axis=1, tiled=True)
    spectra = whitened(arrived)
    width = spectra.shape[1]
    target = second_region[:, 0]
    onehot = (target[:, None] == jnp.arange(regions, dtype=jnp.int32)[None, :]).astype(jnp.int32)
    ranking = jnp.sum((jnp.cumsum(onehot, axis=0) - onehot) * onehot, axis=1)
    slot_index = target * capacity + ranking
    requests = (
        jnp.zeros((regions * capacity,), jnp.int32)
        .at[slot_index]
        .set(second_station)
        .reshape(regions, capacity)
    )
    incoming = lax.all_to_all(requests, "region", split_axis=0, concat_axis=0, tiled=True)
    wanted = jnp.concatenate([first_station, incoming.reshape(-1)])
    initial = jnp.zeros((wanted.shape[0], width), jnp.bfloat16)
    piece = lax.all_gather(spectra, "slab", axis=0, tiled=True)
    inside = (wanted >= 0) & (wanted < piece.shape[0])
    chosen = jnp.take(piece, jnp.clip(wanted, 0, piece.shape[0] - 1), axis=0)
    picked = jnp.where(inside[:, None], chosen, initial)
    first_rows = picked[:pair_count]
    served = picked[pair_count:]
    returned = lax.all_to_all(
        served.reshape(regions, capacity, width), "region", split_axis=0, concat_axis=0, tiled=True
    )
    second_rows = jnp.take(returned.reshape(regions * capacity, width), slot_index, axis=0)
    stacks = cross(first_rows, second_rows)
    return stacks


def solution(mesh):
    placed = (
        P("region", "slab"),
        P(("region", "slab")),
        P(("region", "slab"), None),
        P(("region", "slab")),
    )
    return jax.shard_map(
        local, mesh=mesh, in_specs=placed, out_specs=P(("region", "slab"), None), check_vma=False
    )
```

profile of v0, /device:TPU:32, one launch (start us, length us, event | category | flops | bytes accessed | tf_op | source)
XLA Modules:
  0.0 269.8 jit_solution(3383094113395302440)
XLA Ops:
  6.5 7.3 %all-to-all-start.1 = ((bf16[32,32,128]{2,1,0:T(8,128)(2,1)}), bf16[32,32,128]{2,1,0:T(8,128)(2,1)S(1)}, u32[]{:S(2)}, u32[]{:S(2)}) async-start(bf16[32,32,128]{2,1,0:T(8,128)(2,1)} %bitcast.20), calls=%async_computation.1 | async-start | bytes 524288 | tf_op jit(solution)/shard_map/all_to_all | solution.py:58
  13.9 34.9 %negate_convert_fusion = (bf16[2048,1024]{1,0:T(8,128)(2,1)}, bf16[2048,1024]{1,0:T(8,128)(2,1)}) fusion(), kind=kLoop, calls=%fused_computation.13 | loop fusion | flops 35651584 | bytes 8388608 | tf_op jit(solution)/shard_map/convert.6
  48.9 0.2 convert_reduce_fusion
  49.3 0.1 reduce_sum.61
  49.5 0.3 copy.7
  49.8 0.1 reshape.149
  49.9 4.4 %fusion.3 = f32[64,2048]{1,0:T(8,128)S(1)} fusion(bf16[2048,1024]{1,0:T(8,128)(2,1)} %get-tuple-element.13, bf16[2048,1024]{1,0:T(8,128)(2,1)} %get-tuple-element.14, f32[64,2048]{1,0:T(8,128)S(1)} %reshape.149, f32[2048]{0:T(1024)S(1)} %multiply_subtract_fusion, f32[64]{0:T(128)S(1)} %broadcast_multiply_fusion.1), kind=kOutput, calls=%fused_computation.9 | convolution fusion | flops 554041344 | bytes 9445632 | tf_op jit(solution)/shard_map/dot_general | solution.py:27
  54.3 0.2 fusion.33
  54.5 0.6 fusion.22
  55.2 0.8 reshape.144
  56.1 0.2 reduce_window_sum.11
  56.3 0.2 select_reduce_fusion
  56.5 1.1 scatter_custom_fusion
  57.6 0.7 all_to_all.19
  58.3 15.2 %all-to-all-start = ((s32[16,1,16]{2,1,0:T(1,128)}), s32[16,1,16]{2,1,0:T(1,128)S(1)}, u32[]{:S(2)}, u32[]{:S(2)}) async-start(s32[16,1,16]{2,1,0:T(1,128)} %all_to_all.19), calls=%async_computation | async-start | bytes 16384 | tf_op jit(solution)/shard_map/all_to_all | solution.py:71
  73.5 11.0 %all-to-all-done = s32[16,1,16]{2,1,0:T(1,128)S(1)} async-done(((s32[16,1,16]{2,1,0:T(1,128)}), s32[16,1,16]{2,1,0:T(1,128)S(1)}, u32[]{:S(2)}, u32[]{:S(2)}) %all-to-all-start) | async-done | bytes 1056 | tf_op jit(solution)/shard_map/all_to_all | solution.py:71
  84.6 0.5 broadcast.142
  85.1 0.6 reduce.12
  85.9 42.7 %all-gather.2.cloned.1.call-done = bf16[1024,4096]{1,0:T(8,128)(2,1)} async-done(((bf16[32,4096]{1,0:T(8,128)(2,1)}), bf16[1024,4096]{1,0:T(8,128)(2,1)}) %all-gather.2.cloned.1.call-update) | async-done | bytes 8388624 | tf_op jit(solution)/shard_map/all_gather | solution.py:74
  128.6 12.0 %gather_fusion = bf16[384,4096]{1,0:T(8,128)(2,1)S(1)} fusion(bf16[1024,4096]{1,0:T(8,128)(2,1)} %all-gather.2.cloned.1.call-done, s32[1024]{0:T(1024)S(1)} %pad_clamp_fusion.1), kind=kCustom, calls=%fused_computation | custom fusion | bytes 6292992 | tf_op jit(solution)/shard_map/jit(_take)/gather | solution.py:76
  140.5 0.5 select_select_fusion
  141.0 1.7 copy-done
  142.7 1.5 slice.77
  144.2 12.7 %all-to-all-start.2 = ((bf16[16,16,4096]{2,1,0:T(8,128)(2,1)}), bf16[16,16,4096]{2,1,0:T(8,128)(2,1)S(1)}, u32[]{:S(2)}, u32[]{:S(2)}) async-start(bf16[16,16,4096]{2,1,0:T(8,128)(2,1)} %bitcast.19), calls=%async_computation.2 | async-start | bytes 4194304 | tf_op jit(solution)/shard_map/all_to_all | solution.py:80
  156.9 2.8 %slice_convert_fusion = f32[128,4096]{1,0:T(8,128)} fusion(bf16[384,4096]{1,0:T(8,128)(2,1)} %copy-done), kind=kLoop, calls=%fused_computation.21 | loop fusion | flops 524288 | bytes 3145728 | tf_op jit(solution)/shard_map/reshape | solution.py:43
  159.7 4.0 %reshape.151 = f32[128,2,2,1024]{3,2,1,0:T(2,128)} reshape(f32[128,4096]{1,0:T(8,128)} %slice_convert_fusion) | data formatting | bytes 4194304 | tf_op jit(solution)/shard_map/reshape | solution.py:43
  163.7 87.5 %all-to-all-done.2 = bf16[16,16,4096]{2,1,0:T(8,128)(2,1)S(1)} async-done(((bf16[16,16,4096]{2,1,0:T(8,128)(2,1)}), bf16[16,16,4096]{2,1,0:T(8,128)(2,1)S(1)}, u32[]{:S(2)}, u32[]{:S(2)}) %all-to-all-start.2) | async-done | bytes 2097184 | tf_op jit(solution)/shard_map/all_to_all | solution.py:80
  251.2 1.2 gather_fusion.1
  252.4 1.6 gather.12
  254.0 2.2 fusion.10
  256.2 5.8 %add_reduce_fusion = (f32[128,1024]{1,0:T(8,128)S(1)}, f32[128,1024]{1,0:T(8,128)S(1)}) fusion(f32[128,2,2,1024]{3,2,1,0:T(2,128)S(1)} %fusion.10, f32[128,2,2,1024]{3,2,1,0:T(2,128)S(1)} %copy-done.1), kind=kLoop, calls=%fused_computation.23 | loop fusion | flops 1835008 | bytes 5242880 | tf_op jit(solution)/shard_map/reduce_sum | solution.py:45
  262.1 0.8 pad_maximum_fusion
  (30 shorter events, 0.8 us)
Async XLA Ops:
  6.5 42.4 %all-to-all-start.1 = ((bf16[32,32,128]{2,1,0:T(8,128)(2,1)}), bf16[32,32,128]{2,1,0:T(8,128)(2,1)S(1)}, u32[]{:S(2)}, u32[]{:S(2)}) async-start(bf16[32,32,128]{2,1,0:T(8,128)(2,1)} %bitcast.20), calls=%async_computation.1 | async-start | bytes 524288 | tf_op jit(solution)/shard_map/all_to_all | solution.py:58
  13.9 114.7 %all-gather.2.cloned.1.call-start = ((), (), s32[]{:S(2)}) async-start(), calls=%async_computation.3 | async-start | bytes 8650752 | tf_op jit(solution)/shard_map/all_gather | solution.py:74
  49.9 6.2 %copy-start.2 = (s32[128,1]{0,1:T(1,128)S(1)}, s32[128,1]{0,1:T(1,128)}, u32[]{:S(2)}) copy-start(s32[128,1]{0,1:T(1,128)} %param.6) | copy-start | bytes 1540
  49.9 23.6 %copy-start.3 = (s32[128]{0:T(128)S(1)}, s32[128]{0:T(128)}, u32[]{:S(2)}) copy-start(s32[128]{0:T(128)} %param.5) | copy-start | bytes 1540
  58.3 26.3 %all-to-all-start = ((s32[16,1,16]{2,1,0:T(1,128)}), s32[16,1,16]{2,1,0:T(1,128)S(1)}, u32[]{:S(2)}, u32[]{:S(2)}) async-start(s32[16,1,16]{2,1,0:T(1,128)} %all_to_all.19), calls=%async_computation | async-start | bytes 16384 | tf_op jit(solution)/shard_map/all_to_all | solution.py:71
  141.0 1.7 copy-start
  144.2 107.0 %all-to-all-start.2 = ((bf16[16,16,4096]{2,1,0:T(8,128)(2,1)}), bf16[16,16,4096]{2,1,0:T(8,128)(2,1)S(1)}, u32[]{:S(2)}, u32[]{:S(2)}) async-start(bf16[16,16,4096]{2,1,0:T(8,128)(2,1)} %bitcast.19), calls=%async_computation.2 | async-start | bytes 4194304 | tf_op jit(solution)/shard_map/all_to_all | solution.py:80
  252.4 3.8 %copy-start.1 = (f32[128,2,2,1024]{3,2,1,0:T(2,128)S(1)}, f32[128,2,2,1024]{3,2,1,0:T(2,128)}, u32[]{:S(2)}) copy-start(f32[128,2,2,1024]{3,2,1,0:T(2,128)} %reshape.151) | copy-start | bytes 6291460
Sparse Core Ops, SparseCore 0:
  56.2 72.3 all-gather.1
where the time goes:
time: 270 us
  waiting for transfers between devices  141 us (52%)
  other arithmetic  49.5 us (18%)
  starting transfers between devices  35.2 us (13%)
  local copies, waits for them, and re-layouts  25.8 us (10%)
  between operations  13.6 us (5%)
  matrix products  4.41 us (2%)
    all_to_all x1, waiting for transfers between devices, local(): lax.all_to_all(served.reshape(regions, capacity, width), 'region', split_...  87.5 us
    all_gather x1, waiting for transfers between devices, local(): piece = lax.all_gather(spectra, 'slab', axis=0, tiled=True)  42.7 us
    another operation x3, other arithmetic  35 us
    all_to_all x1, starting transfers between devices, local(): lax.all_to_all(requests, 'region', split_axis=0, concat_axis=0, tiled=True)  15.2 us
    all_to_all x1, starting transfers between devices, local(): lax.all_to_all(served.reshape(regions, capacity, width), 'region', split_...  12.7 us
    gather x1, local copies, waits for them, and re-layouts, local(): chosen = jnp.take(piece, jnp.clip(wanted, 0, piece.shape[0] - 1), axis=0)  12 us
    all_to_all x1, waiting for transfers between devices, local(): lax.all_to_all(requests, 'region', split_axis=0, concat_axis=0, tiled=True)  11 us
    all_to_all x1, starting transfers between devices, local(): lax.all_to_all(records, 'slab', split_axis=0, concat_axis=1, tiled=True)  7.32 us
  transfers between devices with their start and end apart: 4, of which 3 were waited for; matrix products, arithmetic and copies ran while one was open for 17% of the time, Pallas kernels for 0%

commit v1 on v0

--- a/solution.py
+++ b/solution.py
@@ -55,7 +55,13 @@
     regions = lax.axis_size("region")
     pair_count = first_station.shape[0]
     capacity = max(2, pair_count // regions + pair_count // 16)
-    arrived = lax.all_to_all(records, "slab", split_axis=0, concat_axis=1, tiled=True)
+    bands_plan = lambda tile_in, axis_name: jnp.concatenate(
+        lax.all_to_all(
+            jnp.stack(jnp.split(tile_in, lax.axis_size(axis_name), 0), axis=0), axis_name, 0, 0
+        ),
+        1,
+    )
+    arrived = bands_plan(records, "slab")
     spectra = whitened(arrived)
     width = spectra.shape[1]
     target = second_region[:, 0]

time: 270 us -> 313 us (1.16)
  local copies, waits for them, and re-layouts: 25.8 us -> 67.2 us
    unnamed x9 -> x40, local copies, waits for them, and re-layouts: 1.69 us -> 41.8 us
  transfers between devices with their start and end apart: 4 -> 4, of which waited for: 3 -> 3; matrix products, arithmetic and copies ran while one was open for 17% -> 14% of each run, Pallas kernels for 0% -> 0%
where the time goes in v1:
time: 313 us; the launch traced here: 311 us
  waiting for transfers between devices  141 us (45%)
  local copies, waits for them, and re-layouts  67.2 us (21%)
  other arithmetic  49.5 us (16%)
  starting transfers between devices  35.2 us (11%)
  between operations  13.7 us (4%)
  matrix products  4.41 us (1%)
    all_to_all x1, waiting for transfers between devices, local(): lax.all_to_all(served.reshape(regions, capacity, width), 'region', split_...  87.5 us
    all_gather x1, waiting for transfers between devices, local(): piece = lax.all_gather(spectra, 'slab', axis=0, tiled=True)  42.7 us
    unnamed x40, local copies, waits for them, and re-layouts  41.8 us
    another operation x3, other arithmetic  35 us
    all_to_all x1, starting transfers between devices, local(): lax.all_to_all(requests, 'region', split_axis=0, concat_axis=0, tiled=True)  15.2 us
    all_to_all x1, starting transfers between devices, local(): lax.all_to_all(served.reshape(regions, capacity, width), 'region', split_...  12.7 us
    gather x1, local copies, waits for them, and re-layouts, local(): chosen = jnp.take(piece, jnp.clip(wanted, 0, piece.shape[0] - 1), axis=0)  12 us
    all_to_all x1, waiting for transfers between devices, local(): lax.all_to_all(requests, 'region', split_axis=0, concat_axis=0, tiled=True)  11 us
  transfers between devices with their start and end apart: 4, of which 3 were waited for; matrix products, arithmetic and copies ran while one was open for 14% of the time, Pallas kernels for 0%

profile of v1, /device:TPU:32, one launch (start us, length us, event | category | flops | bytes accessed | tf_op | source)
XLA Modules:
  0.0 311.2 jit_solution(10122652128425730091)
XLA Ops:
  6.5 1.3 constant_dynamic-update-slice_fusion.32
  7.8 1.3 constant_dynamic-update-slice_fusion.31
  9.1 1.3 constant_dynamic-update-slice_fusion.30
  10.4 1.3 constant_dynamic-update-slice_fusion.29
  13.0 1.3 constant_dynamic-update-slice_fusion.27
  14.3 1.3 constant_dynamic-update-slice_fusion.26
  15.6 1.3 constant_dynamic-update-slice_fusion.25
  16.9 1.3 constant_dynamic-update-slice_fusion.24
  18.2 1.3 constant_dynamic-update-slice_fusion.23
  20.8 1.3 constant_dynamic-update-slice_fusion.21
  22.1 1.3 constant_dynamic-update-slice_fusion.20
  23.4 1.3 constant_dynamic-update-slice_fusion.19
  24.7 1.3 constant_dynamic-update-slice_fusion.18
  26.0 1.3 constant_dynamic-update-slice_fusion.17
  27.3 1.3 constant_dynamic-update-slice_fusion.16
  29.8 1.3 constant_dynamic-update-slice_fusion.14
  48.0 7.3 %all-to-all-start.1 = ((bf16[32,32,128]{2,1,0:T(8,128)(2,1)}), bf16[32,32,128]{2,1,0:T(8,128)(2,1)S(1)}, u32[]{:S(2)}, u32[]{:S(2)}) async-start(bf16[32,32,128]{2,1,0:T(8,128)(2,1)} %constant_dynamic-update-slice_fusion.1), calls=%async_computation.1 | async-start | bytes 524288 | tf_op jit(solution)/shard_map/all_to_all | solution.py:59
  55.4 34.9 %negate_convert_fusion = (bf16[2048,1024]{1,0:T(8,128)(2,1)}, bf16[2048,1024]{1,0:T(8,128)(2,1)}) fusion(), kind=kLoop, calls=%fused_computation.13 | loop fusion | flops 35651584 | bytes 8388608 | tf_op jit(solution)/shard_map/convert.6
  91.3 4.4 %fusion.3 = f32[64,2048]{1,0:T(8,128)S(1)} fusion(bf16[2048,1024]{1,0:T(8,128)(2,1)} %get-tuple-element.13, bf16[2048,1024]{1,0:T(8,128)(2,1)} %get-tuple-element.14, f32[64,2048]{1,0:T(8,128)S(1)} %reshape.148, f32[2048]{0:T(1024)S(1)} %multiply_subtract_fusion, f32[64]{0:T(128)S(1)} %broadcast_multiply_fusion.1), kind=kOutput, calls=%fused_computation.9 | convolution fusion | flops 554041344 | bytes 9445632 | tf_op jit(solution)/shard_map/dot_general | solution.py:27
  99.7 15.2 %all-to-all-start = ((s32[16,1,16]{2,1,0:T(1,128)}), s32[16,1,16]{2,1,0:T(1,128)S(1)}, u32[]{:S(2)}, u32[]{:S(2)}) async-start(s32[16,1,16]{2,1,0:T(1,128)} %all_to_all.12), calls=%async_computation | async-start | bytes 16384 | tf_op jit(solution)/shard_map/all_to_all | solution.py:77
  115.0 11.0 %all-to-all-done = s32[16,1,16]{2,1,0:T(1,128)S(1)} async-done(((s32[16,1,16]{2,1,0:T(1,128)}), s32[16,1,16]{2,1,0:T(1,128)S(1)}, u32[]{:S(2)}, u32[]{:S(2)}) %all-to-all-start) | async-done | bytes 1056 | tf_op jit(solution)/shard_map/all_to_all | solution.py:77
  127.3 42.7 %all-gather.2.cloned.1.call-done = bf16[1024,4096]{1,0:T(8,128)(2,1)} async-done(((bf16[32,4096]{1,0:T(8,128)(2,1)}), bf16[1024,4096]{1,0:T(8,128)(2,1)}) %all-gather.2.cloned.1.call-update) | async-done | bytes 8388624 | tf_op jit(solution)/shard_map/all_gather | solution.py:80
  170.0 12.0 %gather_fusion = bf16[384,4096]{1,0:T(8,128)(2,1)S(1)} fusion(bf16[1024,4096]{1,0:T(8,128)(2,1)} %all-gather.2.cloned.1.call-done, s32[1024]{0:T(1024)S(1)} %pad_clamp_fusion.1), kind=kCustom, calls=%fused_computation | custom fusion | bytes 6292992 | tf_op jit(solution)/shard_map/jit(_take)/gather | solution.py:82
  182.5 1.7 copy-done
  184.1 1.5 slice.77
  185.6 12.7 %all-to-all-start.2 = ((bf16[16,16,4096]{2,1,0:T(8,128)(2,1)}), bf16[16,16,4096]{2,1,0:T(8,128)(2,1)S(1)}, u32[]{:S(2)}, u32[]{:S(2)}) async-start(bf16[16,16,4096]{2,1,0:T(8,128)(2,1)} %bitcast.82), calls=%async_computation.2 | async-start | bytes 4194304 | tf_op jit(solution)/shard_map/all_to_all | solution.py:86
  198.3 2.8 slice_convert_fusion
  201.1 4.0 %reshape.150 = f32[128,2,2,1024]{3,2,1,0:T(2,128)} reshape(f32[128,4096]{1,0:T(8,128)} %slice_convert_fusion) | data formatting | bytes 4194304 | tf_op jit(solution)/shard_map/reshape | solution.py:43
  205.2 87.5 %all-to-all-done.2 = bf16[16,16,4096]{2,1,0:T(8,128)(2,1)S(1)} async-done(((bf16[16,16,4096]{2,1,0:T(8,128)(2,1)}), bf16[16,16,4096]{2,1,0:T(8,128)(2,1)S(1)}, u32[]{:S(2)}, u32[]{:S(2)}) %all-to-all-start.2) | async-done | bytes 2097184 | tf_op jit(solution)/shard_map/all_to_all | solution.py:86
  293.8 1.6 gather.12
  295.4 2.2 fusion.10
  297.7 5.8 %add_reduce_fusion = (f32[128,1024]{1,0:T(8,128)S(1)}, f32[128,1024]{1,0:T(8,128)S(1)}) fusion(f32[128,2,2,1024]{3,2,1,0:T(2,128)S(1)} %fusion.10, f32[128,2,2,1024]{3,2,1,0:T(2,128)S(1)} %copy-done.1), kind=kLoop, calls=%fused_computation.23 | loop fusion | flops 1835008 | bytes 5242880 | tf_op jit(solution)/shard_map/reduce_sum | solution.py:45
  (62 shorter events, 29.5 us)
Async XLA Ops:
  48.0 42.4 %all-to-all-start.1 = ((bf16[32,32,128]{2,1,0:T(8,128)(2,1)}), bf16[32,32,128]{2,1,0:T(8,128)(2,1)S(1)}, u32[]{:S(2)}, u32[]{:S(2)}) async-start(bf16[32,32,128]{2,1,0:T(8,128)(2,1)} %constant_dynamic-update-slice_fusion.1), calls=%async_computation.1 | async-start | bytes 524288 | tf_op jit(solution)/shard_map/all_to_all | solution.py:59
  55.3 114.7 %all-gather.2.cloned.1.call-start = ((), (), s32[]{:S(2)}) async-start(), calls=%async_computation.3 | async-start | bytes 8650752 | tf_op jit(solution)/shard_map/all_gather | solution.py:80
  91.3 6.2 %copy-start.2 = (s32[128,1]{0,1:T(1,128)S(1)}, s32[128,1]{0,1:T(1,128)}, u32[]{:S(2)}) copy-start(s32[128,1]{0,1:T(1,128)} %param.6) | copy-start | bytes 1540
  91.3 23.6 %copy-start.3 = (s32[128]{0:T(128)S(1)}, s32[128]{0:T(128)}, u32[]{:S(2)}) copy-start(s32[128]{0:T(128)} %param.5) | copy-start | bytes 1540
  99.7 26.3 %all-to-all-start = ((s32[16,1,16]{2,1,0:T(1,128)}), s32[16,1,16]{2,1,0:T(1,128)S(1)}, u32[]{:S(2)}, u32[]{:S(2)}) async-start(s32[16,1,16]{2,1,0:T(1,128)} %all_to_all.12), calls=%async_computation | async-start | bytes 16384 | tf_op jit(solution)/shard_map/all_to_all | solution.py:77
  182.5 1.7 copy-start
  185.6 107.0 %all-to-all-start.2 = ((bf16[16,16,4096]{2,1,0:T(8,128)(2,1)}), bf16[16,16,4096]{2,1,0:T(8,128)(2,1)S(1)}, u32[]{:S(2)}, u32[]{:S(2)}) async-start(bf16[16,16,4096]{2,1,0:T(8,128)(2,1)} %bitcast.82), calls=%async_computation.2 | async-start | bytes 4194304 | tf_op jit(solution)/shard_map/all_to_all | solution.py:86
  293.8 3.8 %copy-start.1 = (f32[128,2,2,1024]{3,2,1,0:T(2,128)S(1)}, f32[128,2,2,1024]{3,2,1,0:T(2,128)}, u32[]{:S(2)}) copy-start(f32[128,2,2,1024]{3,2,1,0:T(2,128)} %reshape.150) | copy-start | bytes 6291460
Sparse Core Ops, SparseCore 0:
  97.6 72.3 all-gather.1
